TPU v7x, 512 devices: a whole 4x4x16 slice. The times are simulated.
512 devices in a mesh: row: 32 (over x, z_lo), col: 16 (over y, z_hi, core).
Axes of the slice: x: 4, y: 4, z: 16 (z_hi: 2, z_lo: 8; z = z_hi * 8 + z_lo), core: 2. Of those that a mesh axis runs over, the one named last changes fastest.
Arguments:
- traces: bfloat16 [32, 2048, 2048], P(None, 'row', 'col'), may hold values from -6 to 6
- source_pos: int32 [2048], P('row'), may hold values from 0 to 16383
- receiver_pos: int32 [2048], replicated, may hold values from 0 to 16383
- aperture_list: int32 [128, 1024], P('row'), may hold values from 0 to 2047, as said below
- band_index: int32 [16384], P('row'), may hold values from 0 to 31
- weight_tiles: bfloat16 [32, 2, 128], replicated, may hold values from -4 to 4
Outputs:
- primaries: bfloat16 [32, 2048, 2048], P(None, 'row', 'col')
- image: float32 [2048, 16384], P('col', 'row')
Inputs may be any that keep to these rules, and one draw needn't show every extreme that they name: `aperture_list`: the 1024 receivers listed for one tile are distinct.
All inputs are finite; a program needn't handle non-finite values.
Results may differ from a plain program's by a relative error of at most 0.012.
Values may be sent and summed in bfloat16 or wider, within the bound.
A program may use at most 64 MiB of HBM per device.

v0:
```python
import math
import jax
import jax.numpy as jnp
from jax import lax
from jax.sharding import PartitionSpec as P

NFFT = 4096
NF = 4


def phase_tables(samples):
    freq_bins = (2 * jnp.arange(NF, dtype=jnp.int32) + 1) * (NFFT // (4 * NF))
    sample_ticks = jnp.arange(samples, dtype=jnp.int32)
    phase_turns = freq_bins[:, None] * sample_ticks[None, :] % NFFT
    phase_angle = phase_turns.astype(jnp.float32) * (2.0 * math.pi / NFFT)
    return (jnp.cos(phase_angle), jnp.sin(phase_angle))


def aperture_matrix(tile_index_lists, positions, columns, first_row, row_count, spread_len):
    tile_count, listed = tile_index_lists.shape
    col_width = columns.shape[0]
    inside = (tile_index_lists >= first_row) & (tile_index_lists < first_row + row_count)
    local_index = jnp.where(inside, tile_index_lists - first_row, row_count)
    tile_rows = jnp.broadcast_to(
        jnp.arange(tile_count, dtype=jnp.int32)[:, None], tile_index_lists.shape
    )
    member = (
        jnp.zeros((tile_count, row_count), jnp.float32)
        .at[tile_rows, local_index]
        .add(1.0, mode="drop")
    )
    widened = jnp.repeat(member.T, col_width // tile_count, axis=1)
    offset = (positions[:, None] - columns[None, :]).astype(jnp.float32) / spread_len
    taper_weight = 1.0 / (1.0 + offset * offset)
    return (widened * taper_weight * (2.0 / math.sqrt(listed))).astype(jnp.bfloat16)


def shot_weights(positions, columns, spread_len):
    offset = (positions[:, None] - columns[None, :]).astype(jnp.float32) / spread_len
    return 1.0 / (1.0 + offset * offset)


def complex_product(left_section, right_section):
    real_real = jnp.einsum(
        "qju,quy->qjy", left_section[0], right_section[0], preferred_element_type=jnp.float32
    )
    imag_imag = jnp.einsum(
        "qju,quy->qjy", left_section[1], right_section[1], preferred_element_type=jnp.float32
    )
    real_imag = jnp.einsum(
        "qju,quy->qjy", left_section[0], right_section[1], preferred_element_type=jnp.float32
    )
    imag_real = jnp.einsum(
        "qju,quy->qjy", left_section[1], right_section[0], preferred_element_type=jnp.float32
    )
    return jnp.stack([real_real - imag_imag, real_imag + imag_real])


def slab_stack(slab_block, aperture, stacking_weights):
    depth_slab_samples, shot_count, listed_rows = slab_block.shape
    stacked = jnp.dot(
        slab_block.reshape(depth_slab_samples * shot_count, listed_rows),
        aperture,
        preferred_element_type=jnp.float32,
    )
    stacked = stacked.reshape(depth_slab_samples, shot_count, aperture.shape[1])
    return jnp.sum(stacked * stacking_weights[None], axis=1)


def per_device(traces, source_pos, receiver_pos, aperture_list, band_index, weight_tiles):
    samples, shot_count, recv_count = traces.shape
    col_count = lax.axis_size("col")
    surface_count = recv_count * col_count
    image_panel_width = band_index.shape[0]
    depth_slab_samples = samples // col_count
    cosine, sine_table = phase_tables(samples)
    forward = (jnp.concatenate([cosine, -sine_table], 0) / math.sqrt(samples)).astype(jnp.bfloat16)
    spectra = jnp.dot(
        forward,
        traces.reshape(samples, shot_count * recv_count),
        preferred_element_type=jnp.float32,
    )
    spectra = spectra.astype(jnp.bfloat16).reshape(2, NF, shot_count, recv_count)
    columns_whole = lax.all_gather(spectra, "row", axis=2, tiled=True)
    summed = complex_product(lax.all_gather(spectra, "col", axis=3, tiled=True), columns_whole)
    multiples = -summed / math.sqrt(surface_count)
    inverse = jnp.concatenate([cosine, -sine_table], 0).T / math.sqrt(NF)
    wave_field = jnp.dot(
        inverse,
        multiples.reshape(2 * NF, shot_count * recv_count),
        precision=lax.Precision.HIGHEST,
        preferred_element_type=jnp.float32,
    )
    primaries = (
        traces.astype(jnp.float32) - wave_field.reshape(samples, shot_count, recv_count)
    ).astype(jnp.bfloat16)
    columns = lax.axis_index("row") * image_panel_width + jnp.arange(
        image_panel_width, dtype=jnp.int32
    )
    spread_len = image_panel_width * lax.axis_size("row") // 4
    stacking_weights = shot_weights(source_pos, columns, spread_len)
    slab_block = lax.all_to_all(primaries, "col", split_axis=0, concat_axis=2, tiled=True)
    aperture = aperture_matrix(aperture_list, receiver_pos, columns, 0, surface_count, spread_len)
    stacked = slab_stack(slab_block, aperture, stacking_weights)
    column_stack = (stacked / math.sqrt(shot_count)).astype(jnp.bfloat16)
    tile_kinds = weight_tiles.shape[0]
    select = band_index[None, :] == jnp.arange(tile_kinds, dtype=jnp.int32)[:, None]
    widened = jnp.where(select[:, None, :], column_stack[None], jnp.zeros((), jnp.bfloat16))
    image_out = jnp.einsum(
        "kz,kx->zx",
        weight_tiles.reshape(tile_kinds * depth_slab_samples, weight_tiles.shape[2]),
        widened.reshape(tile_kinds * depth_slab_samples, image_panel_width),
        preferred_element_type=jnp.float32,
    )
    return (primaries, image_out)


def solution(mesh):
    placed = (P(None, "row", "col"), P("row"), P(), P("row", None), P("row"), P())
    return jax.shard_map(
        per_device,
        mesh=mesh,
        in_specs=placed,
        out_specs=(P(None, "row", "col"), P("col", "row")),
        check_vma=False,
    )
```

profile of v0, /device:TPU:1, one launch (start us, length us, event | category | flops | bytes accessed | tf_op | source)
XLA Modules:
  0.0 404.6 jit_solution(7858936798405555199)
XLA Ops:
  7.4 1.4 fusion.10
  8.8 0.7 copy.33
  9.5 0.7 all-gather.5.cloned.1.call-update
  10.3 0.7 fusion.19
  11.0 0.7 multiply_reduce_fusion
  11.7 0.8 and_reduce_fusion
  12.5 95.1 %all-gather.3.cloned.1.call-done = bf16[2,4,64,2048]{3,2,1,0:T(8,128)(2,1)} async-done(((bf16[2,4,64,128]{3,2,1,0:T(8,128)(2,1)}), bf16[2,4,64,2048]{3,2,1,0:T(8,128)(2,1)}) %all-gather.3.cloned.1.call-update) | async-done | bytes 2097168 | tf_op jit(solution)/shard_map/all_gather | solution.py:85
  107.6 211.9 %all-gather.5.cloned.1.call-done = bf16[2,4,2048,128]{3,2,1,0:T(8,128)(2,1)} async-done(((bf16[2,4,64,128]{3,2,1,0:T(8,128)(2,1)}), bf16[2,4,2048,128]{3,2,1,0:T(8,128)(2,1)}) %all-gather.5.cloned.1.call-update) | async-done | bytes 4194320 | tf_op jit(solution)/shard_map/all_gather | solution.py:84
  319.5 2.5 fusion.1
  322.0 2.4 fusion
  324.5 0.5 fusion.7
  325.0 0.5 fusion.9
  325.5 1.3 fusion.4
  326.8 1.0 copy.30
  327.8 33.6 %all-to-all-start = ((bf16[32,64,128]{2,1,0:T(8,128)(2,1)}), bf16[32,64,128]{2,1,0:T(8,128)(2,1)S(1)}, u32[]{:S(2)}, u32[]{:S(2)}) async-start(bf16[32,64,128]{2,1,0:T(8,128)(2,1)} %copy.30), calls=%async_computation | async-start | bytes 1048576 | tf_op jit(solution)/shard_map/all_to_all | solution.py:102
  361.5 22.1 %scatter_custom_fusion = f32[8192]{0:T(1024)S(1)} fusion(s32[4096]{0:T(1024)S(1)} %bitcast.76, f32[4096]{0:T(1024)S(1)} %broadcast.205, f32[]{:T(128)} %constant.56.clone.1), kind=kCustom, calls=%fused_computation.41 | custom fusion | flops 4096 | bytes 32772
  383.7 0.4 copy.28
  384.1 8.6 %multiply_convert_fusion = bf16[2048,4,128]{2,1,0:T(4,128)(2,1)} fusion(s32[4,128]{1,0:T(4,128)S(1)} %add_add_fusion, s32[2048]{0:T(1024)S(1)} %copy-done.2, f32[2048,4]{1,0:T(8,128)S(1)} %copy.28), kind=kLoop, calls=%fused_computation.2 | loop fusion | flops 9437184 | bytes 2140160 | tf_op jit(solution)/shard_map/convert_element_type | solution.py:35
  392.6 2.7 reshape.161
  395.6 0.3 copy.49
  395.9 0.2 dot_general.40
  396.2 0.5 fusion.5
  396.7 0.2 convolution_bitcast_fusion
  396.9 0.8 copy.31
  (31 shorter events, 0.5 us)
Async XLA Ops:
  7.2 389.5 %copy-start = (bf16[32,2,128]{2,1,0:T(2,128)(2,1)S(1)}, bf16[32,2,128]{2,1,0:T(2,128)(2,1)}, u32[]{:S(2)}) copy-start(bf16[32,2,128]{2,1,0:T(2,128)(2,1)} %param.11) | copy-start | bytes 49156
  7.2 100.4 %all-gather.3.cloned.1.call-start = ((), (), s32[]{:S(2)}) async-start(), calls=%async_computation.1 | async-start | bytes 2228224 | tf_op jit(solution)/shard_map/all_gather | solution.py:85
  9.5 310.0 %all-gather.5.cloned.1.call-start = ((), (), s32[]{:S(2)}) async-start(), calls=%async_computation.2 | async-start | bytes 4325376 | tf_op jit(solution)/shard_map/all_gather | solution.py:84
  107.6 216.9 %copy-start.6 = (bf16[2,4,64,2048]{3,2,1,0:T(8,128)(2,1)S(1)}, bf16[2,4,64,2048]{3,2,1,0:T(8,128)(2,1)}, u32[]{:S(2)}) copy-start(bf16[2,4,64,2048]{3,2,1,0:T(8,128)(2,1)} %all-gather.3.cloned.1.call-done) | copy-start | bytes 6291460
  319.5 5.0 %copy-start.5 = (bf16[2,4,2048,128]{3,2,1,0:T(8,128)(2,1)S(1)}, bf16[2,4,2048,128]{3,2,1,0:T(8,128)(2,1)}, u32[]{:S(2)}) copy-start(bf16[2,4,2048,128]{3,2,1,0:T(8,128)(2,1)} %all-gather.5.cloned.1.call-done) | copy-start | bytes 12582916
  324.5 1.1 copy-start.1
  325.0 59.1 %copy-start.2 = (s32[2048]{0:T(1024)S(1)}, s32[2048]{0:T(1024)}, u32[]{:S(2)}) copy-start(s32[2048]{0:T(1024)} %param.8) | copy-start | bytes 24580
  327.8 67.7 %all-to-all-start = ((bf16[32,64,128]{2,1,0:T(8,128)(2,1)}), bf16[32,64,128]{2,1,0:T(8,128)(2,1)S(1)}, u32[]{:S(2)}, u32[]{:S(2)}) async-start(bf16[32,64,128]{2,1,0:T(8,128)(2,1)} %copy.30), calls=%async_computation | async-start | bytes 1048576 | tf_op jit(solution)/shard_map/all_to_all | solution.py:102
  383.7 11.8 %copy-start.3 = (s32[512]{0:T(512)S(1)}, s32[512]{0:T(512)}, u32[]{:S(2)}) copy-start(s32[512]{0:T(512)} %param.10) | copy-start | bytes 6148
  383.7 11.8 %copy-start.4 = (s32[64]{0:T(128)S(1)}, s32[64]{0:T(128)}, u32[]{:S(2)}) copy-start(s32[64]{0:T(128)} %param.7) | copy-start | bytes 772
Sparse Core Ops, SparseCore 0:
  11.7 95.8 all-gather.2
  110.2 209.1 all-gather.4
where the time goes:
time: 405 us
  waiting for transfers between devices  308 us (76%)
  starting transfers between devices  33.7 us (8%)
  other arithmetic  33.2 us (8%)
  between operations  14.3 us (4%)
  matrix products  9.38 us (2%)
  local copies, waits for them, and re-layouts  6.27 us (2%)
    all_gather x1, waiting for transfers between devices, per_device(): columns_whole = lax.all_gather(spectra, 'row', axis=2, tiled=True)  212 us
    all_gather x1, waiting for transfers between devices, per_device(): lax.all_gather(spectra, 'col', axis=3, tiled=True)  95.1 us
    all_to_all x1, starting transfers between devices, per_device(): lax.all_to_all(primaries, 'col', split_axis=0, concat_axis=2, tiled=True)  33.6 us
    unnamed x4, other arithmetic  23.6 us
    convert_element_type x1, other arithmetic, aperture_matrix(): (widened * taper_weight * (2.0 / math.sqrt(listed))).astype(jnp.bfloat16)  8.57 us
  transfers between devices with their start and end apart: 3, of which 2 were waited for; matrix products, arithmetic and copies ran while one was open for 9% of the time, Pallas kernels for 0%

commit v1 on v0

--- a/solution.py
+++ b/solution.py
@@ -81,7 +81,9 @@
         preferred_element_type=jnp.float32,
     )
     spectra = spectra.astype(jnp.bfloat16).reshape(2, NF, shot_count, recv_count)
-    columns_whole = lax.all_gather(spectra, "row", axis=2, tiled=True)
+    columns_whole = jnp.concatenate(
+        lax.all_to_all(jnp.stack([spectra] * lax.axis_size("row")), "row", 0, 0), axis=2
+    )
     summed = complex_product(lax.all_gather(spectra, "col", axis=3, tiled=True), columns_whole)
     multiples = -summed / math.sqrt(surface_count)
     inverse = jnp.concatenate([cosine, -sine_table], 0).T / math.sqrt(NF)

time: 405 us -> 309 us (0.76)
  the two profiles are of different devices: /device:TPU:1 before, /device:TPU:43 now
where the time goes in v1:
time: 309 us; the launch traced here: 308 us
  waiting for transfers between devices  213 us (69%)
  other arithmetic  31.1 us (10%)
  starting transfers between devices  27 us (9%)
  between operations  14.3 us (5%)
  local copies, waits for them, and re-layouts  14.1 us (5%)
  matrix products  8.1 us (3%)
    all_to_all x1, waiting for transfers between devices, per_device(): lax.all_to_all(jnp.stack([spectra] * lax.axis_size('row')), 'row', 0, 0)  213 us
    unnamed x4, other arithmetic  22.2 us
    all_to_all x1, starting transfers between devices, per_device(): lax.all_to_all(jnp.stack([spectra] * lax.axis_size('row')), 'row', 0, 0)  14.9 us
    all_to_all x1, starting transfers between devices, per_device(): lax.all_to_all(primaries, 'col', split_axis=0, concat_axis=2, tiled=True)  12.1 us
    convert_element_type x1, other arithmetic, aperture_matrix(): (widened * taper_weight * (2.0 / math.sqrt(listed))).astype(jnp.bfloat16)  8.55 us
  transfers between devices with their start and end apart: 3, of which 1 were waited for; matrix products, arithmetic and copies ran while one was open for 13% of the time, Pallas kernels for 0%

profile of v1, /device:TPU:43, one launch (start us, length us, event | category | flops | bytes accessed | tf_op | source)
XLA Modules:
  0.0 308.1 jit_solution(104268075594324993)
XLA Ops:
  7.3 1.4 fusion.2
  8.8 3.0 stack.12
  11.8 14.9 %all-to-all-start = ((bf16[32,2,4,64,128]{4,3,2,1,0:T(8,128)(2,1)}), bf16[32,2,4,64,128]{4,3,2,1,0:T(8,128)(2,1)}, u32[]{:S(2)}, u32[]{:S(2)}) async-start(bf16[32,2,4,64,128]{4,3,2,1,0:T(8,128)(2,1)} %stack.12), calls=%async_computation | async-start | bytes 8388608 | tf_op jit(solution)/shard_map/all_to_all | solution.py:85
  26.8 0.7 all-gather.2.cloned.1.call-update
  27.7 212.8 %all-to-all-done = bf16[32,2,4,64,128]{4,3,2,1,0:T(8,128)(2,1)} async-done(((bf16[32,2,4,64,128]{4,3,2,1,0:T(8,128)(2,1)}), bf16[32,2,4,64,128]{4,3,2,1,0:T(8,128)(2,1)}, u32[]{:S(2)}, u32[]{:S(2)}) %all-to-all-start) | async-done | bytes 4194336 | tf_op jit(solution)/shard_map/all_to_all | solution.py:85
  240.5 3.2 %fusion.32 = (bf16[1,4,32,64,128]{4,3,1,0,2:T(8,128)(2,1)S(1)}, bf16[1,4,32,64,128]{4,3,1,0,2:T(8,128)(2,1)S(1)}) fusion(bf16[2,4,32,64,128]{4,3,1,0,2:T(8,128)(2,1)} %bitcast.2), kind=kLoop, calls=%fused_computation.63 | loop fusion | bytes 8388608 | tf_op jit(solution)/shard_map/slice | solution.py:45
  243.9 1.5 copy.28
  245.4 1.9 fusion.5
  247.3 1.9 fusion.6
  249.2 0.5 fusion.3
  249.8 0.5 fusion.4
  250.3 0.5 copy-done.3
  250.8 1.2 fusion
  252.0 1.0 copy.34
  253.0 12.1 %all-to-all-start.1 = ((bf16[32,64,128]{2,1,0:T(8,128)(2,1)}), bf16[32,64,128]{2,1,0:T(8,128)(2,1)S(1)}, u32[]{:S(2)}, u32[]{:S(2)}) async-start(bf16[32,64,128]{2,1,0:T(8,128)(2,1)} %copy.34), calls=%async_computation.1 | async-start | bytes 1048576 | tf_op jit(solution)/shard_map/all_to_all | solution.py:104
  265.1 22.1 %scatter_custom_fusion = f32[8192]{0:T(1024)S(1)} fusion(s32[4096]{0:T(1024)S(1)} %bitcast.71, f32[4096]{0:T(1024)S(1)} %broadcast.206, f32[]{:T(128)} %constant.56.clone.1), kind=kCustom, calls=%fused_computation.37 | custom fusion | flops 4096 | bytes 32772
  287.2 0.4 copy.32
  287.6 8.5 %multiply_convert_fusion = bf16[2048,4,128]{2,1,0:T(4,128)(2,1)} fusion(s32[4,128]{1,0:T(4,128)S(1)} %add_add_fusion, s32[2048]{0:T(1024)S(1)} %copy-done.6, f32[2048,4]{1,0:T(8,128)S(1)} %copy.32), kind=kLoop, calls=%fused_computation.2 | loop fusion | flops 9437184 | bytes 2140160 | tf_op jit(solution)/shard_map/convert_element_type | solution.py:35
  296.2 2.8 reshape.172
  299.1 0.3 copy.53
  299.5 0.2 dot_general.40
  299.7 0.5 fusion.1
  300.2 0.2 convolution_bitcast_fusion
  300.4 0.8 copy.35
  (42 shorter events, 0.8 us)
Async XLA Ops:
  7.2 293.0 %copy-start = (bf16[32,2,128]{2,1,0:T(2,128)(2,1)S(1)}, bf16[32,2,128]{2,1,0:T(2,128)(2,1)}, u32[]{:S(2)}) copy-start(bf16[32,2,128]{2,1,0:T(2,128)(2,1)} %param.11) | copy-start | bytes 49156
  8.8 3.1 copy-start.4
  11.8 15.6 %copy-start.5 = (s32[4,1024]{1,0:T(4,128)S(1)}, s32[4,1024]{1,0:T(4,128)}, u32[]{:S(2)}) copy-start(s32[4,1024]{1,0:T(4,128)} %param.9) | copy-start | bytes 49156
  11.8 15.7 %copy-start.9 = (s32[2]{0:T(128)S(1)}, s32[2]{0:T(128)}, u32[]{:S(2)}) copy-start(s32[2]{0:T(128)} %constant.68) | copy-start | bytes 28
  11.8 15.8 %copy-start.10 = (s32[2]{0:T(128)S(1)}, s32[2]{0:T(128)}, u32[]{:S(2)}) copy-start(s32[2]{0:T(128)} %constant.71) | copy-start | bytes 28
  11.8 228.6 %all-to-all-start = ((bf16[32,2,4,64,128]{4,3,2,1,0:T(8,128)(2,1)}), bf16[32,2,4,64,128]{4,3,2,1,0:T(8,128)(2,1)}, u32[]{:S(2)}, u32[]{:S(2)}) async-start(bf16[32,2,4,64,128]{4,3,2,1,0:T(8,128)(2,1)} %stack.12), calls=%async_computation | async-start | bytes 8388608 | tf_op jit(solution)/shard_map/all_to_all | solution.py:85
  26.7 218.7 %all-gather.2.cloned.1.call-start = ((), (), s32[]{:S(2)}) async-start(), calls=%async_computation.2 | async-start | bytes 2228224 | tf_op jit(solution)/shard_map/all_gather | solution.py:87
  245.4 1.9 copy-start.1
  247.3 1.9 copy-start.2
  249.7 1.0 copy-start.3
  250.8 36.8 %copy-start.6 = (s32[2048]{0:T(1024)S(1)}, s32[2048]{0:T(1024)}, u32[]{:S(2)}) copy-start(s32[2048]{0:T(1024)} %param.8) | copy-start | bytes 24580
  253.0 46.1 %all-to-all-start.1 = ((bf16[32,64,128]{2,1,0:T(8,128)(2,1)}), bf16[32,64,128]{2,1,0:T(8,128)(2,1)S(1)}, u32[]{:S(2)}, u32[]{:S(2)}) async-start(bf16[32,64,128]{2,1,0:T(8,128)(2,1)} %copy.34), calls=%async_computation.1 | async-start | bytes 1048576 | tf_op jit(solution)/shard_map/all_to_all | solution.py:104
  296.2 2.8 copy-start.7
  296.2 2.8 copy-start.8
Sparse Core Ops, SparseCore 0:
  31.3 97.0 all-gather.1
